TPU v7x, 32 devices: a whole 2x2x4 slice. The times are simulated.
32 devices in a mesh: row: 8 (over z, core), col: 4 (over y, x).
Axes of the slice: x: 2, y: 2, z: 4, core: 2. Of those that a mesh axis runs over, the one named last changes fastest.
Arguments:
- roll_hidden: bfloat16 [1344, 4096], P(('row', 'col')), may hold values from -6 to 6
- roll_cotangent: bfloat16 [1344, 4096], P(('row', 'col')), may hold values from -6 to 6
- lengths: int32 [32], P(('row', 'col')), may hold values from 1 to 42, as said below
- owners: int32 [32], P(('row', 'col')), may hold values from 0 to 7, as said below
- prompts: int32 [32], P(('row', 'col')), may hold values from 0 to 3
- rewards: float32 [32], P(('row', 'col')), may hold values from -5 to 5
- gate_weight: bfloat16 [4096, 14784], P('col', 'row'), may hold values from -0.09375 to 0.09375
- up_weight: bfloat16 [4096, 14784], P('col', 'row'), may hold values from -0.09375 to 0.09375
- down_weight: bfloat16 [14784, 4096], P('row', 'col'), may hold values from -0.046875 to 0.046875
Outputs:
- grad_input: bfloat16 [1024, 4096], P('row', 'col')
- grad_gate: bfloat16 [4096, 14784], P('col', 'row')
- grad_up: bfloat16 [4096, 14784], P('col', 'row')
- grad_down: bfloat16 [14784, 4096], P('row', 'col')
Inputs may be any that keep to these rules, and one draw needn't show every extreme that they name: `owners`: each owner value names exactly 4 rows; the lengths of one owner's rows sum to at most 128, and to exactly 128 for some owner in every draw. `lengths`: some row has length 42 in every draw.
All inputs are finite; a program needn't handle non-finite values.
Results may differ from a plain program's by a relative error of at most 0.025.
Values may be sent and summed in bfloat16 or wider, within the bound.
A program may use at most 128 MiB of HBM per device.

v0:
```python
import jax
import jax.numpy as jnp
from jax import lax
from jax.sharding import PartitionSpec as P

CAPR = 128
spread_floor = 0.7


def row_weights(lengths, prompts, rewards, count_prompts):
    onehot = (prompts[:, None] == jnp.arange(count_prompts, dtype=jnp.int32)[None, :]).astype(
        jnp.float32
    )
    counts = jnp.maximum(jnp.sum(onehot, 0), 1.0)
    means = jnp.sum(onehot * rewards[:, None], 0) / counts
    centred = rewards - jnp.sum(onehot * means[None, :], 1)
    spreads = jnp.sqrt(jnp.sum(onehot * (centred * centred)[:, None], 0) / counts)
    divisor = jnp.maximum(jnp.sum(onehot * spreads[None, :], 1), spread_floor)
    return centred / divisor / lengths.astype(jnp.float32)


def row_offsets(lengths, owners):
    count = lengths.shape[0]
    places = jnp.arange(count, dtype=jnp.int32)
    earlier = (owners[None, :] == owners[:, None]) & (places[None, :] < places[:, None])
    return jnp.sum(jnp.where(earlier, lengths[None, :], 0), 1)


def source_index(lengths, owners, offsets, slot_count, capacity, total):
    count = lengths.shape[0]
    slots = jnp.arange(slot_count, dtype=jnp.int32)
    live = slots[None, :] < lengths[:, None]
    target = jnp.where(live, owners[:, None] * capacity + offsets[:, None] + slots[None, :], total)
    flat_source = slots[None, :] * count + jnp.arange(count, dtype=jnp.int32)[:, None]
    empty = jnp.full((total,), slot_count * count, jnp.int32)
    return empty.at[target.reshape(-1)].set(flat_source.reshape(-1), mode="drop")


def per_device(
    roll_hidden,
    roll_cotangent,
    lengths,
    owners,
    prompts,
    rewards,
    gate_weight,
    up_weight,
    down_weight,
):
    row_count = lax.axis_size("row")
    col_count = lax.axis_size("col")
    total_tokens = row_count * CAPR
    count_prompts = row_count * col_count // 8
    slot_count = roll_hidden.shape[0]
    width = roll_hidden.shape[1] // col_count
    local = jnp.stack(
        [
            lengths.astype(jnp.float32),
            owners.astype(jnp.float32),
            prompts.astype(jnp.float32),
            rewards,
        ],
        axis=1,
    )
    table = lax.all_gather(local, ("row", "col"), axis=0, tiled=True)
    all_lengths = table[:, 0].astype(jnp.int32)
    all_owners = table[:, 1].astype(jnp.int32)
    all_prompts = table[:, 2].astype(jnp.int32)
    weights = row_weights(all_lengths, all_prompts, table[:, 3], count_prompts)
    offsets = row_offsets(all_lengths, all_owners)
    mine = lax.dynamic_slice_in_dim(weights, lax.axis_index(("row", "col")), 1, 0)
    live = (jnp.arange(slot_count, dtype=jnp.int32) < lengths[0])[:, None]
    upstream = jnp.where(live, roll_cotangent.astype(jnp.float32) * mine[0], 0.0).astype(
        jnp.bfloat16
    )
    hidden_blocks = roll_hidden.reshape(slot_count, col_count, width)
    upstream_blocks = upstream.reshape(slot_count, col_count, width)
    hidden_cols, upstream_cols = (
        lax.all_to_all(hidden_blocks, "col", split_axis=1, concat_axis=1, tiled=True),
        lax.all_to_all(upstream_blocks, "col", split_axis=1, concat_axis=1, tiled=True),
    )
    hidden_all, upstream_all = (
        lax.all_gather(hidden_cols, "row", axis=1, tiled=True),
        lax.all_gather(upstream_cols, "row", axis=1, tiled=True),
    )
    sources = source_index(all_lengths, all_owners, offsets, slot_count, CAPR, total_tokens)
    packed = jnp.take(hidden_all.reshape(-1, width), sources, axis=0, mode="fill", fill_value=0)
    packed_grad = jnp.take(
        upstream_all.reshape(-1, width), sources, axis=0, mode="fill", fill_value=0
    )
    gate_term = jnp.dot(packed, gate_weight, preferred_element_type=jnp.float32)
    up_term = jnp.dot(packed, up_weight, preferred_element_type=jnp.float32)
    gate, upval = (
        lax.psum(gate_term.astype(jnp.bfloat16), "col").astype(jnp.float32),
        lax.psum(up_term.astype(jnp.bfloat16), "col").astype(jnp.float32),
    )
    sig = jax.nn.sigmoid(gate)
    silu = gate * sig
    hidden = (silu * upval).astype(jnp.bfloat16)
    contract_cols = (((1,), (1,)), ((), ()))
    grad_term = lax.dot_general(
        packed_grad, down_weight, contract_cols, preferred_element_type=jnp.float32
    )
    grad_hidden = lax.psum(grad_term.astype(jnp.bfloat16), "col").astype(jnp.float32)
    grad_gate_act = (grad_hidden * upval * sig * (1.0 + gate * (1.0 - sig))).astype(jnp.bfloat16)
    grad_up_act = (grad_hidden * silu).astype(jnp.bfloat16)
    contract_rows = (((0,), (0,)), ((), ()))
    grad_down = lax.dot_general(
        hidden, packed_grad, contract_rows, preferred_element_type=jnp.float32
    ).astype(jnp.bfloat16)
    grad_gate = lax.dot_general(
        packed, grad_gate_act, contract_rows, preferred_element_type=jnp.float32
    ).astype(jnp.bfloat16)
    grad_up = lax.dot_general(
        packed, grad_up_act, contract_rows, preferred_element_type=jnp.float32
    ).astype(jnp.bfloat16)
    term = lax.dot_general(
        grad_gate_act, gate_weight, contract_cols, preferred_element_type=jnp.float32
    )
    grad_input = lax.psum_scatter(
        (
            term
            + lax.dot_general(
                grad_up_act, up_weight, contract_cols, preferred_element_type=jnp.float32
            )
        ).astype(jnp.bfloat16),
        "row",
        scatter_dimension=0,
        tiled=True,
    )
    return (grad_input, grad_gate, grad_up, grad_down)


def solution(mesh):
    return jax.shard_map(
        per_device,
        mesh=mesh,
        in_specs=(
            P(("row", "col"), None),
            P(("row", "col"), None),
            P(("row", "col")),
            P(("row", "col")),
            P(("row", "col")),
            P(("row", "col")),
            P("col", "row"),
            P("col", "row"),
            P("row", "col"),
        ),
        out_specs=(P("row", "col"), P("col", "row"), P("col", "row"), P("row", "col")),
        check_vma=False,
    )
```

profile of v0, /device:TPU:0, one launch (start us, length us, event | category | flops | bytes accessed | tf_op | source)
XLA Modules:
  0.0 450.1 jit_solution(12010402054570381515)
XLA Ops:
  7.2 1.2 reshape.123
  8.4 0.1 copy.25
  8.5 12.2 %all_to_all.10 = bf16[42,4,1024]{2,0,1:T(8,128)(2,1)} all-to-all(bf16[42,4,1024]{2,0,1:T(8,128)(2,1)S(1)} %copy.25), channel_id=1, replica_groups=mesh['row'=8,'col'=4] {'col'}, dimensions={1} | all-to-all | bytes 688128 | tf_op jit(solution)/shard_map/all_to_all | solution.py:79
  23.5 66.8 %all-gather = f32[32,1,4]{2,1,0:T(1,128)S(1)} all-gather(f32[1,1,4]{2,1,0:T(1,128)S(1)} %maximum_bitcast_fusion), channel_id=1, replica_groups=mesh['row'=8,'col'=4] {'row','col'}, dimensions={0}, use_global_device_ids=true | all-gather | bytes 528 | tf_op jit(solution)/shard_map/all_gather | solution.py:65
  90.3 0.2 convert_reduce_fusion
  90.6 0.1 select_reduce_fusion.2
  90.8 0.6 dynamic_slice.3
  91.4 1.8 select_convert_fusion
  93.2 0.2 reshape.121
  93.4 0.1 copy.23
  93.5 9.5 %all_to_all.11 = bf16[42,4,1024]{2,0,1:T(8,128)(2,1)} all-to-all(bf16[42,4,1024]{2,0,1:T(8,128)(2,1)S(1)} %copy.23), channel_id=1, replica_groups=mesh['row'=8,'col'=4] {'col'}, dimensions={1} | all-to-all | bytes 688128 | tf_op jit(solution)/shard_map/all_to_all | solution.py:80
  103.1 0.1 reshape.145
  103.2 0.2 select_reduce_fusion
  103.5 0.1 select_n.47
  103.6 7.6 %scatter_custom_fusion = s32[1024]{0:T(1024)S(1)} fusion(s32[1344]{0:T(1024)S(1)} %fusion.15, s32[1344]{0:T(1024)S(1)} %reshape.145, s32[]{:T(128)} %constant.14.clone.1), kind=kCustom, calls=%fused_computation.40 | custom fusion | bytes 4100 | tf_op jit(solution)/shard_map/scatter | solution.py:36
  111.3 3.4 copy.26
  114.7 5.5 %gather_fusion.1 = bf16[1024,1024]{1,0:T(8,128)(2,1)} fusion(bf16[1344,1024]{1,0:T(8,128)(2,1)S(1)} %bitcast.48, s32[1024]{0:T(1024)S(1)} %fusion.16), kind=kCustom, calls=%fused_computation.1.clone | custom fusion | bytes 4198400 | tf_op jit(solution)/shard_map/jit(_take)/gather | solution.py:87
  120.2 17.9 %all-gather.4.cloned.1.call-done = bf16[42,32,1024]{2,0,1:T(8,128)(2,1)} async-done(((bf16[42,4,1024]{2,0,1:T(8,128)(2,1)}), bf16[42,32,1024]{2,0,1:T(8,128)(2,1)}) %all-gather.4.cloned.1.call-update) | async-done | bytes 2752528 | tf_op jit(solution)/shard_map/all_gather | solution.py:84
  138.1 3.4 copy.24
  141.5 5.4 %gather_fusion = bf16[1024,1024]{1,0:T(8,128)(2,1)} fusion(bf16[1344,1024]{1,0:T(8,128)(2,1)S(1)} %bitcast.47, s32[1024]{0:T(1024)S(1)} %fusion.16), kind=kCustom, calls=%fused_computation.clone | custom fusion | bytes 4198400 | tf_op jit(solution)/shard_map/jit(_take)/gather | solution.py:88
  146.8 8.9 %convolution_convert_fusion.2 = bf16[1024,1848]{0,1:T(8,128)(2,1)} fusion(bf16[1024,1848]{0,1:T(8,128)(2,1)} %param.17, bf16[1024,1024]{1,0:T(8,128)(2,1)} %gather_fusion.1, pred[1024]{0:T(1024)(128)(4,1)S(1)} %compare_and_fusion), kind=kOutput, calls=%fused_computation.23 | convolution fusion | flops 3878477824 | bytes 9667584 | tf_op jit(solution)/shard_map/dot_general | solution.py:91
  155.8 6.3 %convolution_convert_fusion.3 = bf16[1024,1848]{0,1:T(8,128)(2,1)} fusion(bf16[1024,1848]{0,1:T(8,128)(2,1)S(1)} %copy-done.11, bf16[1024,1024]{1,0:T(8,128)(2,1)S(1)} %copy-done.6, pred[1024]{0:T(1024)(128)(4,1)S(1)} %compare_and_fusion), kind=kOutput, calls=%fused_computation.24 | convolution fusion | flops 3878477824 | bytes 9667584 | tf_op jit(solution)/shard_map/dot_general | solution.py:92
  162.2 6.3 %convolution_convert_fusion.4 = bf16[1024,1848]{0,1:T(8,128)(2,1)} fusion(bf16[1848,1024]{1,0:T(8,128)(2,1)S(1)} %copy-done.9, bf16[1024,1024]{1,0:T(8,128)(2,1)S(1)} %copy-done.7, pred[1024]{0:T(1024)(128)(4,1)S(1)} %compare_and_fusion), kind=kOutput, calls=%fused_computation.25 | convolution fusion | flops 3878477824 | bytes 9667584 | tf_op jit(solution)/shard_map/dot_general | solution.py:101
  168.6 219.0 %all-reduce.3.cloned.1.call-done = (bf16[1024,1848]{0,1:T(8,128)(2,1)}, bf16[1024,1848]{0,1:T(8,128)(2,1)}, bf16[1024,1848]{0,1:T(8,128)(2,1)}) async-done(((bf16[1024,1848]{0,1:T(8,128)(2,1)}, bf16[1024,1848]{0,1:T(8,128)(2,1)}, bf16[1024,1848]{0,1:T(8,128)(2,1)}), (bf16[1024,1848]{0,1:T(8,128)(2,1)}, bf16[1024,1848]{0,1:T(8,128)(2,1)}, bf16[1024,1848]{0,1:T(8,128)(2,1)})) %all-reduce.3.cloned.1.call-update) | async-done | bytes 11354128 | tf_op jit(solution)/shard_map/psum | solution.py:95
  387.5 6.3 %fusion.3 = bf16[1024,1848]{0,1:T(8,128)(2,1)S(1)} fusion(bf16[1024,1848]{0,1:T(8,128)(2,1)} %get-tuple-element.7, bf16[1024,1848]{0,1:T(8,128)(2,1)} %get-tuple-element.8, bf16[1024,1848]{0,1:T(8,128)(2,1)} %get-tuple-element.9), kind=kLoop, calls=%fused_computation.12 | loop fusion | flops 24600576 | bytes 15138816 | tf_op jit(solution)/shard_map/convert_element_type | solution.py:105
  393.8 1.9 copy-done.5
  395.7 4.7 %fusion.27 = f32[1024,1024]{1,0:T(8,128)S(1)} fusion(bf16[1024,1848]{0,1:T(8,128)(2,1)S(1)} %fusion.3, bf16[1024,1848]{0,1:T(8,128)(2,1)S(1)} %copy-done.10), kind=kOutput, calls=%fused_computation.66 | convolution fusion | flops 3875536896 | bytes 11763712 | tf_op jit(solution)/shard_map/dot_general | solution.py:117
  400.5 6.3 %add_convert_fusion = bf16[1024,1024]{1,0:T(8,128)(2,1)} fusion(f32[1024,1024]{1,0:T(8,128)S(1)} %fusion.27, bf16[1024,1848]{0,1:T(8,128)(2,1)S(1)} %copy-done.12, bf16[1024,1848]{0,1:T(8,128)(2,1)S(1)} %copy-done.3, bf16[1024,1848]{0,1:T(8,128)(2,1)S(1)} %copy-done.1), kind=kOutput, calls=%fused_computation.18 | convolution fusion | flops 3892772864 | bytes 17645568 | tf_op jit(solution)/shard_map/dot_general | solution.py:123
  406.8 7.9 %convolution_convert_fusion.1 = bf16[1024,1848]{0,1:T(8,128)(2,1)} fusion(bf16[1024,1848]{0,1:T(8,128)(2,1)} %copy-done.5, bf16[1024,1024]{1,0:T(8,128)(2,1)S(1)} %copy-done.6, pred[1024]{0:T(1024)(128)(4,1)S(1)} %compare_and_fusion), kind=kOutput, calls=%fused_computation.22 | convolution fusion | flops 3878477824 | bytes 9667584 | tf_op jit(solution)/shard_map/dot_general | solution.py:111
  414.7 6.4 %convolution_convert_fusion = bf16[1024,1848]{0,1:T(8,128)(2,1)} fusion(bf16[1024,1024]{1,0:T(8,128)(2,1)S(1)} %copy-done.6, pred[1024]{0:T(1024)(128)(4,1)S(1)} %compare_and_fusion, bf16[1024,1848]{0,1:T(8,128)(2,1)S(1)} %copy-done.4, bf16[1024,1848]{0,1:T(8,128)(2,1)S(1)} %copy-done.2), kind=kOutput, calls=%fused_computation.21 | convolution fusion | flops 3893616640 | bytes 13452288 | tf_op jit(solution)/shard_map/dot_general | solution.py:114
  421.2 6.4 %fusion.11 = bf16[1848,1024]{1,0:T(8,128)(2,1)} fusion(bf16[1024,1848]{0,1:T(8,128)(2,1)S(1)} %copy-done, bf16[1024,1848]{0,1:T(8,128)(2,1)S(1)} %copy-done.2, bf16[1024,1024]{1,0:T(8,128)(2,1)S(1)} %copy-done.8, pred[1024]{0:T(1024)(128)(4,1)S(1)} %compare_and_fusion), kind=kOutput, calls=%fused_computation.20 | convolution fusion | flops 3893616640 | bytes 13452288 | tf_op jit(solution)/shard_map/dot_general | solution.py:108
  427.6 16.0 %reduce-scatter.2.cloned.1.call-done = bf16[128,1024]{1,0:T(8,128)(2,1)} async-done(((bf16[1024,1024]{1,0:T(8,128)(2,1)}), bf16[128,1024]{1,0:T(8,128)(2,1)}) %reduce-scatter.2.cloned.1.call-update) | async-done | bytes 262160 | tf_op jit(solution)/shard_map/reduce_scatter | solution.py:120
  (51 shorter events, 0.8 us)
Async XLA Ops:
  7.2 104.1 %all-gather.6.cloned.1.call-start = ((), (), s32[]{:S(2)}) async-start(), calls=%async_computation.4 | async-start | bytes 3538944 | tf_op jit(solution)/shard_map/all_gather | solution.py:83
  20.8 117.3 %all-gather.4.cloned.1.call-start = ((), (), s32[]{:S(2)}) async-start(), calls=%async_computation.3 | async-start | bytes 3538944 | tf_op jit(solution)/shard_map/all_gather | solution.py:84
  103.0 284.5 %all-reduce.3.cloned.1.call-start = ((), (), s32[]{:S(2)}) async-start(), calls=%async_computation.6 | async-start | bytes 22708224 | tf_op jit(solution)/shard_map/psum | solution.py:95
  146.8 9.0 %copy-start.6 = (bf16[1024,1024]{1,0:T(8,128)(2,1)S(1)}, bf16[1024,1024]{1,0:T(8,128)(2,1)}, u32[]{:S(2)}) copy-start(bf16[1024,1024]{1,0:T(8,128)(2,1)} %gather_fusion.1) | copy-start | bytes 6291460
  146.8 9.0 %copy-start.11 = (bf16[1024,1848]{0,1:T(8,128)(2,1)S(1)}, bf16[1024,1848]{0,1:T(8,128)(2,1)}, u32[]{:S(2)}) copy-start(bf16[1024,1848]{0,1:T(8,128)(2,1)} %param.18) | copy-start | bytes 11354116
  155.8 6.4 %copy-start.7 = (bf16[1024,1024]{1,0:T(8,128)(2,1)S(1)}, bf16[1024,1024]{1,0:T(8,128)(2,1)}, u32[]{:S(2)}) copy-start(bf16[1024,1024]{1,0:T(8,128)(2,1)} %gather_fusion) | copy-start | bytes 6291460
  155.8 6.4 %copy-start.9 = (bf16[1848,1024]{1,0:T(8,128)(2,1)S(1)}, bf16[1848,1024]{1,0:T(8,128)(2,1)}, u32[]{:S(2)}) copy-start(bf16[1848,1024]{1,0:T(8,128)(2,1)} %param.19) | copy-start | bytes 11354116
  168.5 275.0 %reduce-scatter.2.cloned.1.call-start = ((), (), s32[]{:S(2)}) async-start(), calls=%async_computation.5 | async-start | bytes 2359296 | tf_op jit(solution)/shard_map/reduce_scatter | solution.py:120
  387.5 8.2 %copy-start.10 = (bf16[1024,1848]{0,1:T(8,128)(2,1)S(1)}, bf16[1024,1848]{0,1:T(8,128)(2,1)}, u32[]{:S(2)}) copy-start(bf16[1024,1848]{0,1:T(8,128)(2,1)} %param.17) | copy-start | bytes 11354116
  393.8 1.9 copy-start.5
  395.7 4.8 %copy-start.1 = (bf16[1024,1848]{0,1:T(8,128)(2,1)S(1)}, bf16[1024,1848]{0,1:T(8,128)(2,1)}, u32[]{:S(2)}) copy-start(bf16[1024,1848]{0,1:T(8,128)(2,1)} %get-tuple-element.9) | copy-start | bytes 11354116
  395.7 4.8 %copy-start.3 = (bf16[1024,1848]{0,1:T(8,128)(2,1)S(1)}, bf16[1024,1848]{0,1:T(8,128)(2,1)}, u32[]{:S(2)}) copy-start(bf16[1024,1848]{0,1:T(8,128)(2,1)} %get-tuple-element.8) | copy-start | bytes 11354116
  395.7 4.8 %copy-start.12 = (bf16[1024,1848]{0,1:T(8,128)(2,1)S(1)}, bf16[1024,1848]{0,1:T(8,128)(2,1)}, u32[]{:S(2)}) copy-start(bf16[1024,1848]{0,1:T(8,128)(2,1)} %param.18) | copy-start | bytes 11354116
  406.8 7.9 %copy-start.2 = (bf16[1024,1848]{0,1:T(8,128)(2,1)S(1)}, bf16[1024,1848]{0,1:T(8,128)(2,1)}, u32[]{:S(2)}) copy-start(bf16[1024,1848]{0,1:T(8,128)(2,1)} %get-tuple-element.9) | copy-start | bytes 11354116
  406.8 7.9 %copy-start.4 = (bf16[1024,1848]{0,1:T(8,128)(2,1)S(1)}, bf16[1024,1848]{0,1:T(8,128)(2,1)}, u32[]{:S(2)}) copy-start(bf16[1024,1848]{0,1:T(8,128)(2,1)} %get-tuple-element.8) | copy-start | bytes 11354116
  414.7 6.4 %copy-start = (bf16[1024,1848]{0,1:T(8,128)(2,1)S(1)}, bf16[1024,1848]{0,1:T(8,128)(2,1)}, u32[]{:S(2)}) copy-start(bf16[1024,1848]{0,1:T(8,128)(2,1)} %get-tuple-element.7) | copy-start | bytes 11354116
  414.7 6.4 %copy-start.8 = (bf16[1024,1024]{1,0:T(8,128)(2,1)S(1)}, bf16[1024,1024]{1,0:T(8,128)(2,1)}, u32[]{:S(2)}) copy-start(bf16[1024,1024]{1,0:T(8,128)(2,1)} %gather_fusion) | copy-start | bytes 6291460
Sparse Core Ops, SparseCore 0:
  20.9 37.9 all-gather.5
  103.1 34.8 all-gather.3
  168.6 218.8 all-reduce.2
  406.9 36.5 reduce-scatter.1
where the time goes:
time: 450 us
  waiting for transfers between devices  253 us (56%)
  blocking collectives  88.5 us (20%)
  matrix products  53.4 us (12%)
  local copies, waits for them, and re-layouts  29.7 us (7%)
  between operations  16.6 us (4%)
  other arithmetic  8.91 us (2%)
    psum x1, waiting for transfers between devices, per_device(): lax.psum(up_term.astype(jnp.bfloat16), 'col').astype(jnp.float32)  219 us
    all_gather x1, blocking collectives, per_device(): table = lax.all_gather(local, ('row', 'col'), axis=0, tiled=True)  66.8 us
    all_gather x1, waiting for transfers between devices, per_device(): lax.all_gather(upstream_cols, 'row', axis=1, tiled=True)  17.9 us
    reduce_scatter x1, waiting for transfers between devices, per_device(): lax.psum_scatter((term + lax.dot_general(grad_up_act, up_weight, contract...  16 us
    all_to_all x1, blocking collectives, per_device(): lax.all_to_all(hidden_blocks, 'col', split_axis=1, concat_axis=1, tiled=T...  12.2 us
    all_to_all x1, blocking collectives, per_device(): lax.all_to_all(upstream_blocks, 'col', split_axis=1, concat_axis=1, tiled...  9.51 us
  transfers between devices with their start and end apart: 4, of which 3 were waited for; matrix products, arithmetic and copies ran while one was open for 9% of the time, Pallas kernels for 0%

commit v1 on v0

--- a/solution.py
+++ b/solution.py
@@ -62,7 +62,10 @@
         ],
         axis=1,
     )
-    table = lax.all_gather(local, ("row", "col"), axis=0, tiled=True)
+    table = jnp.concatenate(
+        lax.all_to_all(jnp.stack([local] * lax.axis_size(("row", "col"))), ("row", "col"), 0, 0),
+        axis=0,
+    )
     all_lengths = table[:, 0].astype(jnp.int32)
     all_owners = table[:, 1].astype(jnp.int32)
     all_prompts = table[:, 2].astype(jnp.int32)

time: 450 us -> 397 us (0.88)
  blocking collectives: 88.5 us -> 22.6 us
  waiting for transfers between devices: 253 us -> 258 us
    all_gather x1 -> x0, blocking collectives: 66.8 us -> none  [per_device(): table = lax.all_gather(local, ('row', 'col'), axis=0, tiled=True)]
    all_to_all x0 -> x1, waiting for transfers between devices: none -> 7.09 us  [per_device(): lax.all_to_all(jnp.stack([local] * lax.axis_size(('row', 'col'))), ('row'...]
  transfers between devices with their start and end apart: 4 -> 5, of which waited for: 3 -> 5; matrix products, arithmetic and copies ran while one was open for 9% -> 14% of each run, Pallas kernels for 0% -> 0%
where the time goes in v1:
time: 397 us
  waiting for transfers between devices  258 us (65%)
  matrix products  55.9 us (14%)
  local copies, waits for them, and re-layouts  30.3 us (8%)
  blocking collectives  22.6 us (6%)
  between operations  16.6 us (4%)
  other arithmetic  8.92 us (2%)
  starting transfers between devices  4.48 us (1%)
    psum x1, waiting for transfers between devices, per_device(): lax.psum(up_term.astype(jnp.bfloat16), 'col').astype(jnp.float32)  219 us
    reduce_scatter x1, waiting for transfers between devices, per_device(): lax.psum_scatter((term + lax.dot_general(grad_up_act, up_weight, contract...  16 us
    all_gather x1, waiting for transfers between devices, per_device(): lax.all_gather(upstream_cols, 'row', axis=1, tiled=True)  14.6 us
    all_to_all x1, blocking collectives, per_device(): lax.all_to_all(hidden_blocks, 'col', split_axis=1, concat_axis=1, tiled=T...  12.2 us
    all_to_all x1, blocking collectives, per_device(): lax.all_to_all(upstream_blocks, 'col', split_axis=1, concat_axis=1, tiled...  10.4 us
    dot_general x1, matrix products, per_device(): gate_term = jnp.dot(packed, gate_weight, preferred_element_type=jnp.float32)  8.95 us
    dot_general x1, matrix products, per_device(): lax.dot_general(packed_grad, down_weight, contract_cols, preferred_elemen...  8.8 us
  transfers between devices with their start and end apart: 5, of which 5 were waited for; matrix products, arithmetic and copies ran while one was open for 14% of the time, Pallas kernels for 0%

profile of v1, /device:TPU:0, one launch (start us, length us, event | category | flops | bytes accessed | tf_op | source)
XLA Modules:
  0.0 397.1 jit_solution(16134206368831053686)
XLA Ops:
  7.2 1.2 reshape.130
  8.5 12.2 %all_to_all.15 = bf16[42,4,1024]{2,0,1:T(8,128)(2,1)} all-to-all(bf16[42,4,1024]{2,0,1:T(8,128)(2,1)S(1)} %copy.24), channel_id=1, replica_groups=mesh['row'=8,'col'=4] {'col'}, dimensions={1} | all-to-all | bytes 688128 | tf_op jit(solution)/shard_map/all_to_all | solution.py:82
  23.4 0.6 stack.20
  24.0 4.3 %all-to-all-start = ((f32[32,1,4]{2,1,0:T(1,128)}), f32[32,1,4]{2,1,0:T(1,128)S(1)}, u32[]{:S(2)}, u32[]{:S(2)}) async-start(f32[32,1,4]{2,1,0:T(1,128)} %stack.20), calls=%async_computation | async-start | bytes 32768 | tf_op jit(solution)/shard_map/all_to_all | solution.py:66
  28.4 7.1 %all-to-all-done = f32[32,1,4]{2,1,0:T(1,128)S(1)} async-done(((f32[32,1,4]{2,1,0:T(1,128)}), f32[32,1,4]{2,1,0:T(1,128)S(1)}, u32[]{:S(2)}, u32[]{:S(2)}) %all-to-all-start) | async-done | bytes 544 | tf_op jit(solution)/shard_map/all_to_all | solution.py:66
  35.6 0.2 convert_reduce_fusion
  35.9 0.1 select_reduce_fusion.2
  36.1 0.6 dynamic_slice.3
  36.7 1.8 select_convert_fusion
  38.5 0.2 reshape.128
  38.8 10.4 %all_to_all.16 = bf16[42,4,1024]{2,0,1:T(8,128)(2,1)} all-to-all(bf16[42,4,1024]{2,0,1:T(8,128)(2,1)S(1)} %copy.22), channel_id=1, replica_groups=mesh['row'=8,'col'=4] {'col'}, dimensions={1} | all-to-all | bytes 688128 | tf_op jit(solution)/shard_map/all_to_all | solution.py:83
  49.4 0.2 select_reduce_fusion
  49.7 0.1 select_n.47
  49.8 7.8 %scatter_custom_fusion = s32[1024]{0:T(1024)S(1)} fusion(s32[1344]{0:T(1024)S(1)} %fusion.15, s32[1344]{0:T(1024)S(1)} %reshape.152, s32[]{:T(128)} %constant.14.clone.1), kind=kCustom, calls=%fused_computation.40 | custom fusion | bytes 4100 | tf_op jit(solution)/shard_map/scatter | solution.py:36
  57.7 1.5 all-gather.5.cloned.1.call-done
  59.2 3.4 copy.25
  62.6 5.4 %gather_fusion.1 = bf16[1024,1024]{1,0:T(8,128)(2,1)} fusion(bf16[1344,1024]{1,0:T(8,128)(2,1)S(1)} %bitcast.48, s32[1024]{0:T(1024)S(1)} %fusion.16), kind=kCustom, calls=%fused_computation.1.clone | custom fusion | bytes 4198400 | tf_op jit(solution)/shard_map/jit(_take)/gather | solution.py:90
  68.0 9.0 %convolution_convert_fusion.2 = bf16[1024,1848]{0,1:T(8,128)(2,1)} fusion(bf16[1024,1848]{0,1:T(8,128)(2,1)} %param.17, bf16[1024,1024]{1,0:T(8,128)(2,1)} %gather_fusion.1, pred[1024]{0:T(1024)(128)(4,1)S(1)} %compare_and_fusion), kind=kOutput, calls=%fused_computation.23 | convolution fusion | flops 3878477824 | bytes 9667584 | tf_op jit(solution)/shard_map/dot_general | solution.py:94
  76.9 6.3 %convolution_convert_fusion.3 = bf16[1024,1848]{0,1:T(8,128)(2,1)} fusion(bf16[1024,1848]{0,1:T(8,128)(2,1)S(1)} %copy-done.10, bf16[1024,1024]{1,0:T(8,128)(2,1)S(1)} %copy-done.6, pred[1024]{0:T(1024)(128)(4,1)S(1)} %compare_and_fusion), kind=kOutput, calls=%fused_computation.24 | convolution fusion | flops 3878477824 | bytes 9667584 | tf_op jit(solution)/shard_map/dot_general | solution.py:95
  83.2 14.6 %all-gather.3.cloned.1.call-done = bf16[42,32,1024]{2,0,1:T(8,128)(2,1)} async-done(((bf16[42,4,1024]{2,0,1:T(8,128)(2,1)}), bf16[42,32,1024]{2,0,1:T(8,128)(2,1)}) %all-gather.3.cloned.1.call-update) | async-done | bytes 2752528 | tf_op jit(solution)/shard_map/all_gather | solution.py:87
  97.9 3.4 copy.23
  101.3 5.4 %gather_fusion = bf16[1024,1024]{1,0:T(8,128)(2,1)} fusion(bf16[1344,1024]{1,0:T(8,128)(2,1)S(1)} %bitcast.47, s32[1024]{0:T(1024)S(1)} %fusion.16), kind=kCustom, calls=%fused_computation.clone | custom fusion | bytes 4198400 | tf_op jit(solution)/shard_map/jit(_take)/gather | solution.py:91
  106.6 8.8 %convolution_convert_fusion.4 = bf16[1024,1848]{0,1:T(8,128)(2,1)} fusion(bf16[1848,1024]{1,0:T(8,128)(2,1)} %param.19, bf16[1024,1024]{1,0:T(8,128)(2,1)} %gather_fusion, pred[1024]{0:T(1024)(128)(4,1)S(1)} %compare_and_fusion), kind=kOutput, calls=%fused_computation.25 | convolution fusion | flops 3878477824 | bytes 9667584 | tf_op jit(solution)/shard_map/dot_general | solution.py:104
  115.5 219.0 %all-reduce.3.cloned.1.call-done = (bf16[1024,1848]{0,1:T(8,128)(2,1)}, bf16[1024,1848]{0,1:T(8,128)(2,1)}, bf16[1024,1848]{0,1:T(8,128)(2,1)}) async-done(((bf16[1024,1848]{0,1:T(8,128)(2,1)}, bf16[1024,1848]{0,1:T(8,128)(2,1)}, bf16[1024,1848]{0,1:T(8,128)(2,1)}), (bf16[1024,1848]{0,1:T(8,128)(2,1)}, bf16[1024,1848]{0,1:T(8,128)(2,1)}, bf16[1024,1848]{0,1:T(8,128)(2,1)})) %all-reduce.3.cloned.1.call-update) | async-done | bytes 11354128 | tf_op jit(solution)/shard_map/psum | solution.py:98
  334.5 6.3 %fusion.3 = bf16[1024,1848]{0,1:T(8,128)(2,1)S(1)} fusion(bf16[1024,1848]{0,1:T(8,128)(2,1)} %get-tuple-element.7, bf16[1024,1848]{0,1:T(8,128)(2,1)} %get-tuple-element.8, bf16[1024,1848]{0,1:T(8,128)(2,1)} %get-tuple-element.9), kind=kLoop, calls=%fused_computation.12 | loop fusion | flops 24600576 | bytes 15138816 | tf_op jit(solution)/shard_map/convert_element_type | solution.py:108
  340.8 1.9 copy-done.5
  342.7 4.7 %fusion.27 = f32[1024,1024]{1,0:T(8,128)S(1)} fusion(bf16[1024,1848]{0,1:T(8,128)(2,1)S(1)} %fusion.3, bf16[1024,1848]{0,1:T(8,128)(2,1)S(1)} %copy-done.9), kind=kOutput, calls=%fused_computation.66 | convolution fusion | flops 3875536896 | bytes 11763712 | tf_op jit(solution)/shard_map/dot_general | solution.py:120
  347.4 6.3 %add_convert_fusion = bf16[1024,1024]{1,0:T(8,128)(2,1)} fusion(f32[1024,1024]{1,0:T(8,128)S(1)} %fusion.27, bf16[1024,1848]{0,1:T(8,128)(2,1)S(1)} %copy-done.11, bf16[1024,1848]{0,1:T(8,128)(2,1)S(1)} %copy-done.3, bf16[1024,1848]{0,1:T(8,128)(2,1)S(1)} %copy-done.1), kind=kOutput, calls=%fused_computation.18 | convolution fusion | flops 3892772864 | bytes 17645568 | tf_op jit(solution)/shard_map/dot_general | solution.py:126
  353.8 7.9 %convolution_convert_fusion.1 = bf16[1024,1848]{0,1:T(8,128)(2,1)} fusion(bf16[1024,1848]{0,1:T(8,128)(2,1)} %copy-done.5, bf16[1024,1024]{1,0:T(8,128)(2,1)S(1)} %copy-done.7, pred[1024]{0:T(1024)(128)(4,1)S(1)} %compare_and_fusion), kind=kOutput, calls=%fused_computation.22 | convolution fusion | flops 3878477824 | bytes 9667584 | tf_op jit(solution)/shard_map/dot_general | solution.py:114
  361.7 6.4 %convolution_convert_fusion = bf16[1024,1848]{0,1:T(8,128)(2,1)} fusion(bf16[1024,1024]{1,0:T(8,128)(2,1)S(1)} %copy-done.7, pred[1024]{0:T(1024)(128)(4,1)S(1)} %compare_and_fusion, bf16[1024,1848]{0,1:T(8,128)(2,1)S(1)} %copy-done.4, bf16[1024,1848]{0,1:T(8,128)(2,1)S(1)} %copy-done.2), kind=kOutput, calls=%fused_computation.21 | convolution fusion | flops 3893616640 | bytes 13452288 | tf_op jit(solution)/shard_map/dot_general | solution.py:117
  368.2 6.4 %fusion.11 = bf16[1848,1024]{1,0:T(8,128)(2,1)} fusion(bf16[1024,1848]{0,1:T(8,128)(2,1)S(1)} %copy-done, bf16[1024,1848]{0,1:T(8,128)(2,1)S(1)} %copy-done.2, bf16[1024,1024]{1,0:T(8,128)(2,1)S(1)} %copy-done.8, pred[1024]{0:T(1024)(128)(4,1)S(1)} %compare_and_fusion), kind=kOutput, calls=%fused_computation.20 | convolution fusion | flops 3893616640 | bytes 13452288 | tf_op jit(solution)/shard_map/dot_general | solution.py:111
  374.6 16.0 %reduce-scatter.2.cloned.1.call-done = bf16[128,1024]{1,0:T(8,128)(2,1)} async-done(((bf16[1024,1024]{1,0:T(8,128)(2,1)}), bf16[128,1024]{1,0:T(8,128)(2,1)}) %reduce-scatter.2.cloned.1.call-update) | async-done | bytes 262160 | tf_op jit(solution)/shard_map/reduce_scatter | solution.py:123
  (51 shorter events, 1.1 us)
Async XLA Ops:
  7.2 52.0 %all-gather.5.cloned.1.call-start = ((), (), s32[]{:S(2)}) async-start(), calls=%async_computation.5 | async-start | bytes 3538944 | tf_op jit(solution)/shard_map/all_gather | solution.py:86
  24.0 11.5 %all-to-all-start = ((f32[32,1,4]{2,1,0:T(1,128)}), f32[32,1,4]{2,1,0:T(1,128)S(1)}, u32[]{:S(2)}, u32[]{:S(2)}) async-start(f32[32,1,4]{2,1,0:T(1,128)} %stack.20), calls=%async_computation | async-start | bytes 32768 | tf_op jit(solution)/shard_map/all_to_all | solution.py:66
  28.4 69.5 %all-gather.3.cloned.1.call-start = ((), (), s32[]{:S(2)}) async-start(), calls=%async_computation.4 | async-start | bytes 3538944 | tf_op jit(solution)/shard_map/all_gather | solution.py:87
  49.2 285.3 %all-reduce.3.cloned.1.call-start = ((), (), s32[]{:S(2)}) async-start(), calls=%async_computation.7 | async-start | bytes 22708224 | tf_op jit(solution)/shard_map/psum | solution.py:98
  68.0 9.0 %copy-start.6 = (bf16[1024,1024]{1,0:T(8,128)(2,1)S(1)}, bf16[1024,1024]{1,0:T(8,128)(2,1)}, u32[]{:S(2)}) copy-start(bf16[1024,1024]{1,0:T(8,128)(2,1)} %gather_fusion.1) | copy-start | bytes 6291460
  68.0 9.0 %copy-start.10 = (bf16[1024,1848]{0,1:T(8,128)(2,1)S(1)}, bf16[1024,1848]{0,1:T(8,128)(2,1)}, u32[]{:S(2)}) copy-start(bf16[1024,1848]{0,1:T(8,128)(2,1)} %param.18) | copy-start | bytes 11354116
  115.5 275.1 %reduce-scatter.2.cloned.1.call-start = ((), (), s32[]{:S(2)}) async-start(), calls=%async_computation.6 | async-start | bytes 2359296 | tf_op jit(solution)/shard_map/reduce_scatter | solution.py:123
  334.5 8.2 %copy-start.9 = (bf16[1024,1848]{0,1:T(8,128)(2,1)S(1)}, bf16[1024,1848]{0,1:T(8,128)(2,1)}, u32[]{:S(2)}) copy-start(bf16[1024,1848]{0,1:T(8,128)(2,1)} %param.17) | copy-start | bytes 11354116
  340.8 1.9 copy-start.5
  342.6 4.8 %copy-start.1 = (bf16[1024,1848]{0,1:T(8,128)(2,1)S(1)}, bf16[1024,1848]{0,1:T(8,128)(2,1)}, u32[]{:S(2)}) copy-start(bf16[1024,1848]{0,1:T(8,128)(2,1)} %get-tuple-element.9) | copy-start | bytes 11354116
  342.6 4.8 %copy-start.3 = (bf16[1024,1848]{0,1:T(8,128)(2,1)S(1)}, bf16[1024,1848]{0,1:T(8,128)(2,1)}, u32[]{:S(2)}) copy-start(bf16[1024,1848]{0,1:T(8,128)(2,1)} %get-tuple-element.8) | copy-start | bytes 11354116
  342.6 4.8 %copy-start.11 = (bf16[1024,1848]{0,1:T(8,128)(2,1)S(1)}, bf16[1024,1848]{0,1:T(8,128)(2,1)}, u32[]{:S(2)}) copy-start(bf16[1024,1848]{0,1:T(8,128)(2,1)} %param.18) | copy-start | bytes 11354116
  347.4 6.4 %copy-start.7 = (bf16[1024,1024]{1,0:T(8,128)(2,1)S(1)}, bf16[1024,1024]{1,0:T(8,128)(2,1)}, u32[]{:S(2)}) copy-start(bf16[1024,1024]{1,0:T(8,128)(2,1)} %gather_fusion.1) | copy-start | bytes 6291460
  353.8 7.9 %copy-start.2 = (bf16[1024,1848]{0,1:T(8,128)(2,1)S(1)}, bf16[1024,1848]{0,1:T(8,128)(2,1)}, u32[]{:S(2)}) copy-start(bf16[1024,1848]{0,1:T(8,128)(2,1)} %get-tuple-element.9) | copy-start | bytes 11354116
  353.8 7.9 %copy-start.4 = (bf16[1024,1848]{0,1:T(8,128)(2,1)S(1)}, bf16[1024,1848]{0,1:T(8,128)(2,1)}, u32[]{:S(2)}) copy-start(bf16[1024,1848]{0,1:T(8,128)(2,1)} %get-tuple-element.8) | copy-start | bytes 11354116
  361.7 6.5 %copy-start = (bf16[1024,1848]{0,1:T(8,128)(2,1)S(1)}, bf16[1024,1848]{0,1:T(8,128)(2,1)}, u32[]{:S(2)}) copy-start(bf16[1024,1848]{0,1:T(8,128)(2,1)} %get-tuple-element.7) | copy-start | bytes 11354116
  361.7 6.4 %copy-start.8 = (bf16[1024,1024]{1,0:T(8,128)(2,1)S(1)}, bf16[1024,1024]{1,0:T(8,128)(2,1)}, u32[]{:S(2)}) copy-start(bf16[1024,1024]{1,0:T(8,128)(2,1)} %gather_fusion) | copy-start | bytes 6291460
Sparse Core Ops, SparseCore 0:
  20.9 38.2 all-gather.4
  60.8 37.0 all-gather.2
  115.6 218.8 all-reduce.2
  353.9 36.5 reduce-scatter.1
